TPU v7x, 32 devices: a whole 2x2x4 slice. The times are simulated.
32 devices in a mesh: tile: 8 (over y, x, core), mode: 4 (over z).
Axes of the slice: x: 2, y: 2, z: 4, core: 2. Of those that a mesh axis runs over, the one named last changes fastest.
Arguments:
- object_field: float32 [2, 2, 2048, 384], P(None, None, 'tile'), may hold values from -4 to 4
- probe: float32 [8, 2, 256, 256], P('mode'), may hold values from -4 to 4
- measured: float32 [32, 256, 256], P('tile'), may hold values from 0 to 16
- prop_phase: float32 [256, 256], replicated, may hold values from -3.140625 to 3.140625
- counts: int32 [8], P('tile'), may hold values from 1 to 4, 16 in all
- row_offset: int32 [32], P('tile'), may hold values from 0 to 255
- col_offset: int32 [32], P('tile'), may hold values from 0 to 128
Outputs:
- object_grad: float32 [2, 2, 2048, 384], P(None, None, 'tile')
- probe_grad: float32 [8, 2, 256, 256], P('mode')
Inputs may be any that keep to these rules, and one draw needn't show every extreme that they name: Slot i is live for i % 4 < counts[i // 4]; some tile has all 4 slots live.
All inputs are finite; a program needn't handle non-finite values. No bound on the sum of `counts` on one device may be relied on, other than what follows from the above.
Results may differ from a plain program's by a relative error of at most 0.0003.
Values sent between devices are 32-bit elements; how exact they have to be, the bound alone decides.
A program may use at most 128 MiB of HBM per device.

v0:
```python
import math
import jax
import jax.numpy as jnp
from jax import lax
from jax.sharding import PartitionSpec as P

MODES = 8
HIGH = lax.Precision.HIGHEST


def shifted(block, axis, distance):
    devices = range(lax.axis_size(axis))
    route = [(i - distance, i) for i in devices if i - distance in devices]
    return lax.ppermute(block, axis, route)


def dft_tables(length):
    indices = jnp.arange(length, dtype=jnp.int32)
    product = indices[:, None] * indices[None, :] % length
    angle = product.astype(jnp.float32) * (2.0 * math.pi / length)
    factor = 1.0 / math.sqrt(length)
    return (jnp.cos(angle) * factor, jnp.sin(angle) * factor)


def on_left(matrix, field):
    return jnp.einsum("jk,mkl->mjl", matrix, field, precision=HIGH)


def on_right(field, matrix):
    return jnp.einsum("mjk,kl->mjl", field, matrix, precision=HIGH)


def transform(pair, tables, sign):
    cosine, sine = tables
    real_in, imag_in = pair
    mid_real = on_left(cosine, real_in) - sign * on_left(sine, imag_in)
    mid_imag = on_left(cosine, imag_in) + sign * on_left(sine, real_in)
    out_real = on_right(mid_real, cosine) - sign * on_right(mid_imag, sine)
    out_imag = on_right(mid_imag, cosine) + sign * on_right(mid_real, sine)
    return (out_real, out_imag)


def times(first, second):
    return (
        first[0] * second[0] - first[1] * second[1],
        first[0] * second[1] + first[1] * second[0],
    )


def times_conj(first, second):
    return (
        first[0] * second[0] + first[1] * second[1],
        first[0] * second[1] - first[1] * second[0],
    )


def forward_pass(window, probe_pair, kernel, tables):
    wave = times(probe_pair, (window[0, 0], window[0, 1]))
    spectrum = transform(wave, tables, -1.0)
    moved = transform(times(kernel, spectrum), tables, 1.0)
    before = [moved]
    wave = times(moved, (window[1, 0], window[1, 1]))
    far_field = transform(wave, tables, -1.0)
    return (before, far_field)


def backward_pass(window, before, far_field, weight, probe_pair, kernel, tables):
    layers = window.shape[0]
    back = transform((weight * far_field[0], weight * far_field[1]), tables, 1.0)
    pieces = [None] * layers
    term = times_conj(before[0], back)
    pieces[1] = jnp.stack([jnp.sum(term[0], axis=0), jnp.sum(term[1], axis=0)])
    inner = transform(times_conj((window[1, 0], window[1, 1]), back), tables, -1.0)
    back = transform(times_conj(kernel, inner), tables, 1.0)
    first = times_conj(probe_pair, back)
    pieces[0] = jnp.stack([jnp.sum(first[0], axis=0), jnp.sum(first[1], axis=0)])
    probe_term = times_conj((window[0, 0], window[0, 1]), back)
    return (jnp.stack(pieces), jnp.stack([probe_term[0], probe_term[1]], axis=1))


def per_device(object_field, probe, measured, prop_phase, counts, row_offset, col_offset):
    layers, _, tile_rows, columns = object_field.shape
    width = probe.shape[-1]
    next_rows = shifted(object_field, "tile", -1)
    extended = jnp.concatenate([object_field, next_rows], axis=2)
    tables = dft_tables(width)
    kernel = (jnp.cos(prop_phase), jnp.sin(prop_phase))
    probe_pair = (probe[:, 0], probe[:, 1])
    live_count = counts[0]
    zero_index = jnp.zeros((), jnp.int32)
    slot_total = row_offset.shape[0]

    def cut_window(row_start, col_start):
        start = (zero_index, zero_index, row_start, col_start)
        return lax.dynamic_slice(extended, start, (layers, 2, width, width))

    def place_terms(grad_ext, pieces, row_start, col_start):
        start = (zero_index, zero_index, row_start, col_start)
        current = lax.dynamic_slice(grad_ext, start, (layers, 2, width, width))
        return lax.dynamic_update_slice(grad_ext, current + pieces, start)

    init = (jnp.zeros(extended.shape, jnp.float32), jnp.zeros(probe.shape, jnp.float32))
    windows = jax.vmap(cut_window)(row_offset, col_offset)
    before, far_field = jax.vmap(lambda item: forward_pass(item, probe_pair, kernel, tables))(
        windows
    )
    local_power = jnp.sum(far_field[0] * far_field[0] + far_field[1] * far_field[1], axis=1)
    power = lax.psum(local_power, "mode")
    alive = (jnp.arange(slot_total, dtype=jnp.int32) < live_count).astype(jnp.float32)
    weight = (power - measured) / MODES * alive[:, None, None]

    def one_back(item, item_before, item_far, item_weight):
        return backward_pass(item, item_before, item_far, item_weight, probe_pair, kernel, tables)

    all_pieces, probe_terms = jax.vmap(one_back)(windows, before, far_field, weight)
    grad_probe = jnp.sum(probe_terms, axis=0)

    def add_slot(slot, grad_ext):
        return place_terms(grad_ext, all_pieces[slot], row_offset[slot], col_offset[slot])

    grad_ext = lax.fori_loop(zero_index, jnp.full((), slot_total, jnp.int32), add_slot, init[0])
    summed = lax.psum(grad_ext, "mode")
    arrived = shifted(summed[:, :, tile_rows:, :], "tile", 1)
    object_grad = summed[:, :, :tile_rows, :].at[:, :, :width, :].add(arrived)
    probe_grad = lax.psum(grad_probe, "tile")
    return (object_grad, probe_grad)


def solution(mesh):
    placed = (
        P(None, None, "tile", None),
        P("mode", None, None, None),
        P("tile", None, None),
        P(),
        P("tile"),
        P("tile"),
        P("tile"),
    )
    return jax.shard_map(
        per_device,
        mesh=mesh,
        in_specs=placed,
        out_specs=(P(None, None, "tile", None), P("mode", None, None, None)),
        check_vma=False,
    )
```

profile of v0, /device:TPU:0, one launch (start us, length us, event | category | flops | bytes accessed | tf_op | source)
XLA Modules:
  0.0 612.1 jit_solution(3632968894506634922)
XLA Ops:
  10.1 2.6 fusion.421
  16.6 12.5 %while.14 = (s32[]{:T(128)}, f32[2,2,512,384]{3,2,1,0:T(8,128)S(1)}, s32[4,4]{1,0:T(4,128)S(1)}, f32[4,2,2,256,256]{4,3,2,1,0:T(8,128)}, s32[]{:T(128)}) while((s32[]{:T(128)}, f32[2,2,512,384]{3,2,1,0:T(8,128)S(1)}, s32[4,4]{1,0:T(4,128)S(1)}, f32[4,2,2,256,256]{4,3,2,1,0:T(8,128)}, s32[]{:T(128)}) %tuple.57), condition=%wide.while_cond.1, body=%wide.while_body.1.sunk | while | flops 2 | bytes 2098801 | solution.py:95
  20.4 2.5 bitcast_dynamic-update-slice_fusion.2
  26.6 2.5 bitcast_dynamic-update-slice_fusion.2
  29.2 2.7 slice_bitcast_fusion.3
  31.9 4.5 fusion.49
  36.4 4.4 fusion.48
  40.8 4.6 multiply_add_fusion.9
  45.4 4.3 fusion.40
  49.8 4.3 fusion.42
  54.1 4.7 multiply_subtract_fusion.9
  58.8 4.5 multiply_add_fusion.8
  63.2 4.8 multiply_subtract_fusion.8
  68.1 4.6 fusion.116
  72.7 4.6 fusion.117
  77.3 4.8 convolution_add_fusion.1
  82.1 4.5 fusion.34
  86.6 4.5 fusion.32
  91.0 4.8 convolution_subtract_fusion.1
  95.9 4.5 fusion.70
  100.3 4.5 fusion.73
  104.8 5.0 fusion.165
  109.9 4.6 fusion.162
  114.5 4.8 multiply_add_fusion.5
  119.3 4.5 fusion.26
  123.8 4.5 fusion.24
  128.3 4.8 multiply_subtract_fusion.5
  133.1 4.5 multiply_subtract_fusion.4
  137.6 7.2 %add_reduce_fusion.2 = (f32[4,256,256]{2,1,0:T(8,128)}, f32[4,2,256,256]{3,2,1,0:T(8,128)}) fusion(f32[4,2,256,256]{3,2,1,0:T(8,128)S(1)} %multiply_subtract_fusion.4, f32[4,2,256,256]{3,2,1,0:T(8,128)S(1)} %fusion.24, f32[4,2,256,256]{3,2,1,0:T(8,128)S(1)} %multiply_subtract_fusion.5), kind=kOutput, calls=%fused_computation.70 | convolution fusion | flops 1614479360 | bytes 9437184 | tf_op jit(solution)/shard_map/vmap(mjk,kl->mjl)/dot_general | solution.py:30
  145.9 67.4 %all-reduce.4.cloned.1.call-done = f32[4,256,256]{2,1,0:T(8,128)} async-done(((f32[4,256,256]{2,1,0:T(8,128)}), f32[4,256,256]{2,1,0:T(8,128)}) %all-reduce.4.cloned.1.call-update) | async-done | bytes 1048592 | tf_op jit(solution)/shard_map/psum | solution.py:108
  215.5 4.5 fusion.54
  220.0 4.5 fusion.52
  224.5 4.7 fusion.63
  229.2 4.6 fusion.18
  233.8 4.6 fusion.16
  238.3 4.7 fusion.60
  243.1 4.5 fusion.80
  247.6 5.6 add_reduce_fusion
  253.2 4.6 fusion.155
  257.8 4.6 fusion.152
  262.5 4.8 multiply_add_fusion.2
  267.3 4.5 fusion.8
  271.8 4.5 fusion.10
  276.3 4.9 multiply_subtract_fusion.2
  281.2 4.6 multiply_add_fusion.1
  285.8 4.6 multiply_subtract_fusion.1
  290.4 5.0 fusion.118
  295.4 4.6 fusion.119
  300.0 4.8 convolution_add_fusion
  304.8 4.5 fusion.2
  309.3 4.5 fusion
  313.8 4.9 convolution_subtract_fusion
  318.7 4.5 fusion.90
  323.2 7.6 %add_bitcast_fusion = (f32[4,2,1,256,256]{4,3,1,0,2:T(8,128)S(1)}, f32[4,2,1,256,256]{4,3,1,0,2:T(8,128)}, f32[4,256,256]{2,1,0:T(8,128)S(1)}, f32[4,256,256]{2,1,0:T(8,128)S(1)}) fusion(f32[4,2,256,256]{3,2,1,0:T(8,128)S(1)} %fusion.90, f32[4,256,256]{2,1,0:T(8,128)S(1)} %get-tuple-element.89, f32[4,256,256]{2,1,0:T(8,128)S(1)} %copy-done.5, ...), kind=kOutput, calls=%fused_computation.57 | convolution fusion | flops 1618935808 | bytes 15728640 | tf_op jit(solution)/shard_map/vmap(mjk,kl->mjl)/dot_general | solution.py:30
  335.3 75.1 %while.13 = (s32[]{:T(128)}, f32[2,2,512,384]{3,2,1,0:T(8,128)}, s32[4]{0:T(128)S(1)}, s32[4]{0:T(128)S(1)}, f32[4,2,2,256,256]{4,3,2,1,0:T(8,128)}, /*index=5*/s32[]{:T(128)}, s32[]{:T(128)}, s32[]{:T(128)}, s32[]{:T(128)}) while((s32[]{:T(128)}, f32[2,2,512,384]{3,2,1,0:T(8,128)}, s32[4]{0:T(128)S(1)}, s32[4]{0:T(128)S(1)}, ...), condition=%wide.region_7.8_spmd, body=%wide.region_6.7_spmd.sunk | while | flops 262152 | bytes 5243081 | solution.py:121
  342.4 11.9 %dynamic_update_slice.4 = f32[2,2,512,384]{3,2,1,0:T(8,128)} dynamic-update-slice(f32[2,2,512,384]{3,2,1,0:T(8,128)} %get-tuple-element.186, f32[2,2,256,256]{3,2,1,0:T(8,128)S(1)} %bitcast_add_fusion.2, s32[]{:T(128)} %constant.72.clone.1..sunk, s32[]{:T(128)} %constant.72.clone.1..sunk, s32[]{:T(128)S(6)} %select_n.288, s32[]{:T(128)S(6)} %select_n.289) | dynamic-update-slice | bytes 2097156 | tf_op jit(solution)/shard_map/while/body/dynamic_update_slice | solution.py:100
  361.6 11.7 %dynamic_update_slice.4 = f32[2,2,512,384]{3,2,1,0:T(8,128)} dynamic-update-slice(f32[2,2,512,384]{3,2,1,0:T(8,128)} %get-tuple-element.186, f32[2,2,256,256]{3,2,1,0:T(8,128)S(1)} %bitcast_add_fusion.2, s32[]{:T(128)} %constant.72.clone.1..sunk, s32[]{:T(128)} %constant.72.clone.1..sunk, s32[]{:T(128)S(6)} %select_n.288, s32[]{:T(128)S(6)} %select_n.289) | dynamic-update-slice | bytes 2097156 | tf_op jit(solution)/shard_map/while/body/dynamic_update_slice | solution.py:100
  380.4 11.6 %dynamic_update_slice.4 = f32[2,2,512,384]{3,2,1,0:T(8,128)} dynamic-update-slice(f32[2,2,512,384]{3,2,1,0:T(8,128)} %get-tuple-element.186, f32[2,2,256,256]{3,2,1,0:T(8,128)S(1)} %bitcast_add_fusion.2, s32[]{:T(128)} %constant.72.clone.1..sunk, s32[]{:T(128)} %constant.72.clone.1..sunk, s32[]{:T(128)S(6)} %select_n.288, s32[]{:T(128)S(6)} %select_n.289) | dynamic-update-slice | bytes 2097156 | tf_op jit(solution)/shard_map/while/body/dynamic_update_slice | solution.py:100
  399.1 11.3 %dynamic_update_slice.4 = f32[2,2,512,384]{3,2,1,0:T(8,128)} dynamic-update-slice(f32[2,2,512,384]{3,2,1,0:T(8,128)} %get-tuple-element.186, f32[2,2,256,256]{3,2,1,0:T(8,128)S(1)} %bitcast_add_fusion.2, s32[]{:T(128)} %constant.72.clone.1..sunk, s32[]{:T(128)} %constant.72.clone.1..sunk, s32[]{:T(128)S(6)} %select_n.288, s32[]{:T(128)S(6)} %select_n.289) | dynamic-update-slice | bytes 2097156 | tf_op jit(solution)/shard_map/while/body/dynamic_update_slice | solution.py:100
  410.5 120.5 %all-reduce.6.cloned.1.call-done = f32[2,2,512,384]{3,2,1,0:T(8,128)} async-done(((f32[2,2,512,384]{3,2,1,0:T(8,128)}), f32[2,2,512,384]{3,2,1,0:T(8,128)}) %all-reduce.6.cloned.1.call-update) | async-done | bytes 3145744 | tf_op jit(solution)/shard_map/psum | solution.py:122
  530.9 2.8 slice.80
  533.7 2.7 collective-permute-start.1
  537.8 62.4 %all-reduce.8.cloned.1.call-done = f32[2,2,256,256]{3,2,0,1:T(8,128)} async-done(((f32[2,2,256,256]{3,2,0,1:T(8,128)}), f32[2,2,256,256]{3,2,0,1:T(8,128)}) %all-reduce.8.cloned.1.call-update) | async-done | bytes 1048592 | tf_op jit(solution)/shard_map/psum | solution.py:125
  602.5 2.7 slice_add_fusion
  (88 shorter events, 38.2 us)
Async XLA Ops:
  7.2 206.1 %all-reduce.4.cloned.1.call-start = ((), (), s32[]{:S(2)}) async-start(), calls=%async_computation | async-start | bytes 2097152 | tf_op jit(solution)/shard_map/psum | solution.py:108
  7.2 7.8 %collective-permute-start = (f32[2,2,256,384]{3,2,1,0:T(8,128)}, f32[2,2,256,384]{3,2,1,0:T(8,128)}, u32[]{:S(2)}, u32[]{:S(2)}) collective-permute-start(f32[2,2,256,384]{3,2,1,0:T(8,128)} %param.13), channel_id=1, source_target_pairs={{4,0},{8,4},{12,8},{16,12},{20,16},{24,20},{28,24},{5,1},{9,5},{13... | collective-permute-start | bytes 4718600 | tf_op jit(solution)/shard_map/ppermute | solution.py:14
  10.0 5.0 copy-start.17
  29.2 2.7 copy-start.10
  29.2 2.7 copy-start.12
  31.9 22.2 %copy-start.4 = (f32[4,256,256]{2,1,0:T(8,128)}, f32[4,256,256]{2,1,0:T(8,128)S(1)}, u32[]{:S(2)}) copy-start(f32[4,256,256]{2,1,0:T(8,128)S(1)} %get-tuple-element.90) | copy-start | bytes 3145732
  63.2 4.9 copy-start.8
  100.3 27.9 %copy-start = (f32[4,2,256,256]{3,2,1,0:T(8,128)}, f32[4,2,256,256]{3,2,1,0:T(8,128)S(1)}, u32[]{:S(2)}) copy-start(f32[4,2,256,256]{3,2,1,0:T(8,128)S(1)} %fusion.70) | copy-start | bytes 6291460
  104.8 23.4 %copy-start.2 = (f32[4,2,256,256]{3,2,1,0:T(8,128)}, f32[4,2,256,256]{3,2,1,0:T(8,128)S(1)}, u32[]{:S(2)}) copy-start(f32[4,2,256,256]{3,2,1,0:T(8,128)S(1)} %fusion.73) | copy-start | bytes 6291460
  137.6 7.2 %copy-start.6 = (f32[4,2,256,256]{3,2,1,0:T(8,128)}, f32[4,2,256,256]{3,2,1,0:T(8,128)S(1)}, u32[]{:S(2)}) copy-start(f32[4,2,256,256]{3,2,1,0:T(8,128)S(1)} %multiply_subtract_fusion.4) | copy-start | bytes 6291460
  144.8 386.1 %all-reduce.6.cloned.1.call-start = ((), (), s32[]{:S(2)}) async-start(), calls=%async_computation.1 | async-start | bytes 6291456 | tf_op jit(solution)/shard_map/psum | solution.py:122
  213.3 2.2 copy-start.14
  220.0 4.5 copy-start.7
  243.1 4.5 copy-start.1
  243.1 4.5 copy-start.3
  285.8 4.6 copy-start.9
  318.7 4.5 copy-start.5
  318.7 4.5 copy-start.11
  318.7 4.5 copy-start.13
  333.4 1.9 copy-start.18
  333.4 1.9 copy-start.19
  410.4 189.7 %all-reduce.8.cloned.1.call-start = ((), (), s32[]{:S(2)}) async-start(), calls=%async_computation.2 | async-start | bytes 2097152 | tf_op jit(solution)/shard_map/psum | solution.py:125
  530.9 5.5 copy-start.15
  533.7 68.7 %collective-permute-start.1 = (f32[2,2,256,384]{3,2,1,0:T(8,128)}, f32[2,2,256,384]{3,2,1,0:T(8,128)}, u32[]{:S(2)}, u32[]{:S(2)}) collective-permute-start(f32[2,2,256,384]{3,2,1,0:T(8,128)} %slice.80), channel_id=1, source_target_pairs={{0,4},{4,8},{8,12},{12,16},{16,20},{20,24},{24,28},{1,5},{5,9},{9,... | collective-permute-start | bytes 4718600 | tf_op jit(solution)/shard_map/ppermute | solution.py:14
  537.7 64.7 %copy-start.16 = (f32[2,2,512,384]{3,2,1,0:T(8,128)S(1)}, f32[2,2,512,384]{3,2,1,0:T(8,128)}, u32[]{:S(2)}) copy-start(f32[2,2,512,384]{3,2,1,0:T(8,128)} %all-reduce.6.cloned.1.call-done) | copy-start | bytes 9437188
Sparse Core Ops, SparseCore 0:
  144.9 68.2 all-reduce.3
  410.6 120.3 all-reduce.5
  537.9 62.2 all-reduce.7
where the time goes:
time: 624 us; the launch traced here: 612 us
  waiting for transfers between devices  250 us (40%)
  matrix products  228 us (37%)
  local copies, waits for them, and re-layouts  78.8 us (13%)
  other arithmetic  19.9 us (3%)
  loops' own time  15.6 us (2%)
  between operations  15.4 us (2%)
    psum x1, waiting for transfers between devices, per_device(): summed = lax.psum(grad_ext, 'mode')  120 us
    dot_general x24, matrix products, on_right(): return jnp.einsum('mjk,kl->mjl', field, matrix, precision=HIGH)  115 us
    dot_general x24, matrix products, on_left(): return jnp.einsum('jk,mkl->mjl', matrix, field, precision=HIGH)  113 us
    psum x1, waiting for transfers between devices, per_device(): power = lax.psum(local_power, 'mode')  67.4 us
    psum x1, waiting for transfers between devices, per_device(): probe_grad = lax.psum(grad_probe, 'tile')  62.4 us
    dynamic_update_slice x4, local copies, waits for them, and re-layouts, place_terms(): return lax.dynamic_update_slice(grad_ext, current + pieces, start)  46.5 us
    another operation x1, loops' own time, per_device(): lax.fori_loop(zero_index, jnp.full((), slot_total, jnp.int32), add_slot,...  15.6 us
    gather x12, local copies, waits for them, and re-layouts  12.5 us
  transfers between devices with their start and end apart: 5, of which 3 were waited for; matrix products, arithmetic and copies ran while one was open for 2% of the time, Pallas kernels for 0%

commit v1 on v0

--- a/solution.py
+++ b/solution.py
@@ -105,7 +105,7 @@
         windows
     )
     local_power = jnp.sum(far_field[0] * far_field[0] + far_field[1] * far_field[1], axis=1)
-    power = lax.psum(local_power, "mode")
+    power = jnp.sum(lax.all_gather(local_power, "mode"), axis=0)
     alive = (jnp.arange(slot_total, dtype=jnp.int32) < live_count).astype(jnp.float32)
     weight = (power - measured) / MODES * alive[:, None, None]
 

time: 624 us -> 655 us (1.050)
  waiting for transfers between devices: 250 us -> 278 us
    all_gather x0 -> x1, waiting for transfers between devices: none -> 96.1 us  [per_device(): power = jnp.sum(lax.all_gather(local_power, 'mode'), axis=0)]
    psum x1 -> x0, waiting for transfers between devices: 67.4 us -> none  [per_device(): power = lax.psum(local_power, 'mode')]
where the time goes in v1:
time: 655 us; the launch traced here: 644 us
  waiting for transfers between devices  278 us (42%)
  matrix products  228 us (35%)
  local copies, waits for them, and re-layouts  78.9 us (12%)
  other arithmetic  23.5 us (4%)
  loops' own time  15.6 us (2%)
  between operations  15.5 us (2%)
    psum x1, waiting for transfers between devices, per_device(): summed = lax.psum(grad_ext, 'mode')  120 us
    dot_general x24, matrix products, on_right(): return jnp.einsum('mjk,kl->mjl', field, matrix, precision=HIGH)  115 us
    dot_general x24, matrix products, on_left(): return jnp.einsum('jk,mkl->mjl', matrix, field, precision=HIGH)  112 us
    all_gather x1, waiting for transfers between devices, per_device(): power = jnp.sum(lax.all_gather(local_power, 'mode'), axis=0)  96.1 us
    psum x1, waiting for transfers between devices, per_device(): probe_grad = lax.psum(grad_probe, 'tile')  62.4 us
    dynamic_update_slice x4, local copies, waits for them, and re-layouts, place_terms(): return lax.dynamic_update_slice(grad_ext, current + pieces, start)  46.5 us
    another operation x1, loops' own time, per_device(): lax.fori_loop(zero_index, jnp.full((), slot_total, jnp.int32), add_slot,...  15.6 us
  transfers between devices with their start and end apart: 5, of which 3 were waited for; matrix products, arithmetic and copies ran while one was open for 2% of the time, Pallas kernels for 0%

profile of v1, /device:TPU:0, one launch (start us, length us, event | category | flops | bytes accessed | tf_op | source)
XLA Modules:
  0.0 643.8 jit_solution(3595766616273387384)
XLA Ops:
  10.1 2.6 fusion.421
  16.7 12.5 %while.14 = (s32[]{:T(128)}, f32[2,2,512,384]{3,2,1,0:T(8,128)S(1)}, s32[4,4]{1,0:T(4,128)S(1)}, f32[4,2,2,256,256]{4,3,2,1,0:T(8,128)}, s32[]{:T(128)}) while((s32[]{:T(128)}, f32[2,2,512,384]{3,2,1,0:T(8,128)S(1)}, s32[4,4]{1,0:T(4,128)S(1)}, f32[4,2,2,256,256]{4,3,2,1,0:T(8,128)}, s32[]{:T(128)}) %tuple.57), condition=%wide.while_cond.1, body=%wide.while_body.1.sunk | while | flops 2 | bytes 2098801 | solution.py:95
  20.4 2.5 bitcast_dynamic-update-slice_fusion.2
  29.2 2.7 slice_bitcast_fusion.3
  32.0 4.5 fusion.49
  36.5 4.4 fusion.48
  40.9 4.6 multiply_add_fusion.9
  45.5 4.3 fusion.40
  49.8 4.3 fusion.42
  54.2 4.7 multiply_subtract_fusion.9
  58.8 4.5 multiply_add_fusion.8
  63.3 4.8 multiply_subtract_fusion.8
  68.2 4.6 fusion.116
  72.8 4.6 fusion.117
  77.4 4.8 convolution_add_fusion.1
  82.2 4.5 fusion.34
  86.6 4.5 fusion.32
  91.1 4.8 convolution_subtract_fusion.1
  95.9 4.5 fusion.70
  100.4 4.5 fusion.73
  104.9 5.0 fusion.165
  109.9 4.6 fusion.162
  114.6 4.8 multiply_add_fusion.5
  119.4 4.5 fusion.26
  123.8 4.5 fusion.24
  128.3 4.8 multiply_subtract_fusion.5
  133.2 4.5 multiply_subtract_fusion.4
  137.7 7.2 %add_reduce_fusion.2 = (f32[4,256,256]{2,1,0:T(8,128)}, f32[4,2,256,256]{3,2,1,0:T(8,128)}) fusion(f32[4,2,256,256]{3,2,1,0:T(8,128)S(1)} %multiply_subtract_fusion.4, f32[4,2,256,256]{3,2,1,0:T(8,128)S(1)} %fusion.24, f32[4,2,256,256]{3,2,1,0:T(8,128)S(1)} %multiply_subtract_fusion.5), kind=kOutput, calls=%fused_computation.70 | convolution fusion | flops 1614479360 | bytes 9437184 | tf_op jit(solution)/shard_map/vmap(mjk,kl->mjl)/dot_general | solution.py:30
  146.0 96.1 %all-gather.3.cloned.1.call-done = f32[16,256,256]{2,1,0:T(8,128)} async-done(((f32[4,256,256]{2,1,0:T(8,128)}), f32[16,256,256]{2,1,0:T(8,128)}) %all-gather.3.cloned.1.call-update) | async-done | bytes 4194320 | tf_op jit(solution)/shard_map/all_gather | solution.py:108
  242.1 3.6 reduce_sum.64
  247.9 4.5 fusion.54
  252.4 4.5 fusion.52
  256.9 4.7 fusion.63
  261.6 4.6 fusion.18
  266.2 4.6 fusion.16
  270.7 4.7 fusion.60
  275.5 4.5 fusion.80
  280.0 5.6 add_reduce_fusion
  285.6 4.6 fusion.155
  290.2 4.6 fusion.152
  294.9 4.8 multiply_add_fusion.2
  299.7 4.5 fusion.8
  304.2 4.5 fusion.10
  308.7 4.9 multiply_subtract_fusion.2
  313.6 4.6 multiply_add_fusion.1
  318.2 5.0 multiply_subtract_fusion.1
  323.2 4.6 fusion.118
  327.8 4.6 fusion.119
  332.4 4.8 convolution_add_fusion
  337.2 4.5 fusion.2
  341.7 4.5 fusion
  346.2 4.9 convolution_subtract_fusion
  351.1 4.5 fusion.90
  355.6 7.6 %add_bitcast_fusion = (f32[4,2,1,256,256]{4,3,1,0,2:T(8,128)S(1)}, f32[4,2,1,256,256]{4,3,1,0,2:T(8,128)}, f32[4,256,256]{2,1,0:T(8,128)S(1)}, f32[4,256,256]{2,1,0:T(8,128)S(1)}) fusion(f32[4,2,256,256]{3,2,1,0:T(8,128)S(1)} %fusion.90, f32[4,256,256]{2,1,0:T(8,128)S(1)} %get-tuple-element.89, f32[4,256,256]{2,1,0:T(8,128)S(1)} %copy-done.5, ...), kind=kOutput, calls=%fused_computation.57 | convolution fusion | flops 1618935808 | bytes 15728640 | tf_op jit(solution)/shard_map/vmap(mjk,kl->mjl)/dot_general | solution.py:30
  367.7 75.1 %while.13 = (s32[]{:T(128)}, f32[2,2,512,384]{3,2,1,0:T(8,128)}, s32[4]{0:T(128)S(1)}, s32[4]{0:T(128)S(1)}, f32[4,2,2,256,256]{4,3,2,1,0:T(8,128)}, /*index=5*/s32[]{:T(128)}, s32[]{:T(128)}, s32[]{:T(128)}, s32[]{:T(128)}) while((s32[]{:T(128)}, f32[2,2,512,384]{3,2,1,0:T(8,128)}, s32[4]{0:T(128)S(1)}, s32[4]{0:T(128)S(1)}, ...), condition=%wide.region_7.8_spmd, body=%wide.region_6.7_spmd.sunk | while | flops 262152 | bytes 5243081 | solution.py:121
  374.8 11.9 %dynamic_update_slice.4 = f32[2,2,512,384]{3,2,1,0:T(8,128)} dynamic-update-slice(f32[2,2,512,384]{3,2,1,0:T(8,128)} %get-tuple-element.186, f32[2,2,256,256]{3,2,1,0:T(8,128)S(1)} %bitcast_add_fusion.2, s32[]{:T(128)} %constant.72.clone.1..sunk, s32[]{:T(128)} %constant.72.clone.1..sunk, s32[]{:T(128)S(6)} %select_n.288, s32[]{:T(128)S(6)} %select_n.289) | dynamic-update-slice | bytes 2097156 | tf_op jit(solution)/shard_map/while/body/dynamic_update_slice | solution.py:100
  394.0 11.7 %dynamic_update_slice.4 = f32[2,2,512,384]{3,2,1,0:T(8,128)} dynamic-update-slice(f32[2,2,512,384]{3,2,1,0:T(8,128)} %get-tuple-element.186, f32[2,2,256,256]{3,2,1,0:T(8,128)S(1)} %bitcast_add_fusion.2, s32[]{:T(128)} %constant.72.clone.1..sunk, s32[]{:T(128)} %constant.72.clone.1..sunk, s32[]{:T(128)S(6)} %select_n.288, s32[]{:T(128)S(6)} %select_n.289) | dynamic-update-slice | bytes 2097156 | tf_op jit(solution)/shard_map/while/body/dynamic_update_slice | solution.py:100
  412.8 11.6 %dynamic_update_slice.4 = f32[2,2,512,384]{3,2,1,0:T(8,128)} dynamic-update-slice(f32[2,2,512,384]{3,2,1,0:T(8,128)} %get-tuple-element.186, f32[2,2,256,256]{3,2,1,0:T(8,128)S(1)} %bitcast_add_fusion.2, s32[]{:T(128)} %constant.72.clone.1..sunk, s32[]{:T(128)} %constant.72.clone.1..sunk, s32[]{:T(128)S(6)} %select_n.288, s32[]{:T(128)S(6)} %select_n.289) | dynamic-update-slice | bytes 2097156 | tf_op jit(solution)/shard_map/while/body/dynamic_update_slice | solution.py:100
  431.5 11.3 %dynamic_update_slice.4 = f32[2,2,512,384]{3,2,1,0:T(8,128)} dynamic-update-slice(f32[2,2,512,384]{3,2,1,0:T(8,128)} %get-tuple-element.186, f32[2,2,256,256]{3,2,1,0:T(8,128)S(1)} %bitcast_add_fusion.2, s32[]{:T(128)} %constant.72.clone.1..sunk, s32[]{:T(128)} %constant.72.clone.1..sunk, s32[]{:T(128)S(6)} %select_n.288, s32[]{:T(128)S(6)} %select_n.289) | dynamic-update-slice | bytes 2097156 | tf_op jit(solution)/shard_map/while/body/dynamic_update_slice | solution.py:100
  442.9 119.7 %all-reduce.3.cloned.1.call-done = f32[2,2,512,384]{3,2,1,0:T(8,128)} async-done(((f32[2,2,512,384]{3,2,1,0:T(8,128)}), f32[2,2,512,384]{3,2,1,0:T(8,128)}) %all-reduce.3.cloned.1.call-update) | async-done | bytes 3145744 | tf_op jit(solution)/shard_map/psum | solution.py:122
  562.6 2.8 slice.80
  565.4 2.7 collective-permute-start.1
  569.4 62.4 %all-reduce.5.cloned.1.call-done = f32[2,2,256,256]{3,2,0,1:T(8,128)} async-done(((f32[2,2,256,256]{3,2,0,1:T(8,128)}), f32[2,2,256,256]{3,2,0,1:T(8,128)}) %all-reduce.5.cloned.1.call-update) | async-done | bytes 1048592 | tf_op jit(solution)/shard_map/psum | solution.py:125
  634.1 2.7 slice_add_fusion
  (89 shorter events, 40.8 us)
Async XLA Ops:
  7.2 234.9 %all-gather.3.cloned.1.call-start = ((), (), s32[]{:S(2)}) async-start(), calls=%async_computation.2 | async-start | bytes 5242880 | tf_op jit(solution)/shard_map/all_gather | solution.py:108
  7.2 7.9 %collective-permute-start = (f32[2,2,256,384]{3,2,1,0:T(8,128)}, f32[2,2,256,384]{3,2,1,0:T(8,128)}, u32[]{:S(2)}, u32[]{:S(2)}) collective-permute-start(f32[2,2,256,384]{3,2,1,0:T(8,128)} %param.13), channel_id=1, source_target_pairs={{4,0},{8,4},{12,8},{16,12},{20,16},{24,20},{28,24},{5,1},{9,5},{13... | collective-permute-start | bytes 4718600 | tf_op jit(solution)/shard_map/ppermute | solution.py:14
  10.0 5.0 copy-start.17
  29.2 2.7 copy-start.10
  29.2 2.7 copy-start.12
  31.9 22.2 %copy-start.4 = (f32[4,256,256]{2,1,0:T(8,128)}, f32[4,256,256]{2,1,0:T(8,128)S(1)}, u32[]{:S(2)}) copy-start(f32[4,256,256]{2,1,0:T(8,128)S(1)} %get-tuple-element.90) | copy-start | bytes 3145732
  63.3 4.9 copy-start.8
  100.4 27.9 %copy-start = (f32[4,2,256,256]{3,2,1,0:T(8,128)}, f32[4,2,256,256]{3,2,1,0:T(8,128)S(1)}, u32[]{:S(2)}) copy-start(f32[4,2,256,256]{3,2,1,0:T(8,128)S(1)} %fusion.70) | copy-start | bytes 6291460
  104.9 23.4 %copy-start.2 = (f32[4,2,256,256]{3,2,1,0:T(8,128)}, f32[4,2,256,256]{3,2,1,0:T(8,128)S(1)}, u32[]{:S(2)}) copy-start(f32[4,2,256,256]{3,2,1,0:T(8,128)S(1)} %fusion.73) | copy-start | bytes 6291460
  137.7 7.2 %copy-start.6 = (f32[4,2,256,256]{3,2,1,0:T(8,128)}, f32[4,2,256,256]{3,2,1,0:T(8,128)S(1)}, u32[]{:S(2)}) copy-start(f32[4,2,256,256]{3,2,1,0:T(8,128)S(1)} %multiply_subtract_fusion.4) | copy-start | bytes 6291460
  144.9 417.7 %all-reduce.3.cloned.1.call-start = ((), (), s32[]{:S(2)}) async-start(), calls=%async_computation | async-start | bytes 6291456 | tf_op jit(solution)/shard_map/psum | solution.py:122
  245.7 2.2 copy-start.14
  252.4 4.5 copy-start.7
  275.5 4.5 copy-start.1
  275.5 4.5 copy-start.3
  318.2 5.0 copy-start.9
  351.1 4.5 copy-start.5
  351.1 4.5 copy-start.11
  351.1 4.5 copy-start.13
  365.8 1.9 copy-start.18
  365.8 1.9 copy-start.19
  442.8 189.0 %all-reduce.5.cloned.1.call-start = ((), (), s32[]{:S(2)}) async-start(), calls=%async_computation.1 | async-start | bytes 2097152 | tf_op jit(solution)/shard_map/psum | solution.py:125
  562.6 5.5 copy-start.15
  565.4 68.7 %collective-permute-start.1 = (f32[2,2,256,384]{3,2,1,0:T(8,128)}, f32[2,2,256,384]{3,2,1,0:T(8,128)}, u32[]{:S(2)}, u32[]{:S(2)}) collective-permute-start(f32[2,2,256,384]{3,2,1,0:T(8,128)} %slice.80), channel_id=1, source_target_pairs={{0,4},{4,8},{8,12},{12,16},{16,20},{20,24},{24,28},{1,5},{5,9},{9,... | collective-permute-start | bytes 4718600 | tf_op jit(solution)/shard_map/ppermute | solution.py:14
  569.4 64.7 %copy-start.16 = (f32[2,2,512,384]{3,2,1,0:T(8,128)S(1)}, f32[2,2,512,384]{3,2,1,0:T(8,128)}, u32[]{:S(2)}) copy-start(f32[2,2,512,384]{3,2,1,0:T(8,128)} %all-reduce.3.cloned.1.call-done) | copy-start | bytes 9437188
Sparse Core Ops, SparseCore 0:
  145.0 97.0 all-gather.2
  443.0 119.5 all-reduce.2
  569.5 62.2 all-reduce.4
